TPU v7x, 128 devices: a whole 4x4x4 slice. The times are simulated.
128 devices in a mesh: by: 8 (over z, core), bx: 16 (over x, y).
Axes of the slice: x: 4, y: 4, z: 4, core: 2. Of those that a mesh axis runs over, the one named last changes fastest.
Arguments:
- tracers: float32 [20, 512, 16, 2048], P(None, ('by', 'bx')), may hold values from 0 to 1
- vertical_speed: float32 [20, 512, 2048], P(None, ('by', 'bx')), may hold values from -0.4 to 0.4
- diffusivity: float32 [20, 512, 2048], P(None, ('by', 'bx')), may hold values from 0.02 to 2
- buoyancy_force: bfloat16 [20, 512, 2048], P(None, ('by', 'bx')), may hold values from -2.1 to 2.1
- wet_levels: int32 [512, 2048], P(('by', 'bx')), may hold values from 0 to 20
- surface_patch: int32 [512, 2048], P(('by', 'bx')), may hold values from 0 to 15
- prior_height: float32 [512, 2048], P(('by', 'bx')), may hold values from -5 to 5
- land_mask: int32 [512, 16, 128], P(('by', 'bx')), may hold values 0 or 1
- baroclinic_map: int32 [512], replicated, may hold values from 0 to 511, as said below
- barotropic_map: int32 [512], replicated, may hold values from 0 to 511, as said below
Outputs:
- new_tracers: float32 [20, 512, 16, 2048], P(None, ('by', 'bx'))
- surface_height: float32 [512, 16, 128], P(('by', 'bx'))
Inputs may be any that keep to these rules, and one draw needn't show every extreme that they name: baroclinic_map[s] is the geographic block held in baroclinic slot s, blocks numbered row by row with 64 to a block row; it lies in block row s // 64, and every block appears once. barotropic_map[s] is the geographic block held in barotropic slot s, blocks numbered row by row with 64 to a block row; it lies in block row s // 64, and every block appears once.
All inputs are finite; a program needn't handle non-finite values. No bound on the sum of `land_mask` on one device may be relied on, other than what follows from the above.
Results may differ from a plain program's by a relative error of at most 0.0003.
Values sent between devices are 32-bit elements; how exact they have to be, the bound alone decides.
A program may use at most 128 MiB of HBM per device.

v0:
```python
import jax
import jax.numpy as jnp
from jax import lax
from jax.sharding import PartitionSpec as P

ITERS = 6
RESTORE = 0.5
SURFACE = 0.1
FACE_SCALE = 2.0
PRECISE = lax.Precision.HIGHEST


def padded_2(block, sides, width):
    for axis, dim in sides:
        count = lax.axis_size(axis)
        forward = [(i, i + 1) for i in range(count - 1)]
        backward = [(target, source) for source, target in forward]
        low = lax.ppermute(
            lax.slice_in_dim(block, block.shape[dim] - width, None, axis=dim), axis, forward
        )
        high = lax.ppermute(lax.slice_in_dim(block, 0, width, axis=dim), axis, backward)
        block = jnp.concatenate([low, block, high], axis=dim)
    return block


def column_step(tracers, vertical_speed, diffusivity, wet_levels, surface_patch):
    depth_index = lax.broadcasted_iota(jnp.int32, vertical_speed.shape, 0)
    wet_level = (depth_index < wet_levels[None]).astype(jnp.float32)
    open_faces = (depth_index + 1 < wet_levels[None]).astype(jnp.float32)
    speed_open = (vertical_speed * open_faces)[:, :, None]
    shifted_up = jnp.concatenate([tracers[1:], jnp.zeros_like(tracers[:1])], axis=0)
    flux_below = jnp.maximum(speed_open, 0.0) * shifted_up + jnp.minimum(speed_open, 0.0) * tracers
    flux_above = jnp.concatenate([jnp.zeros_like(flux_below[:1]), flux_below[:-1]], axis=0)
    advected = wet_level[:, :, None] * (tracers + flux_below - flux_above)
    mixing = diffusivity * open_faces
    mixing_above = jnp.concatenate([jnp.zeros_like(mixing[:1]), mixing[:-1]], axis=0)
    surface_row = (depth_index == 0).astype(jnp.float32) * wet_level * RESTORE
    diagonal = 1.0 + mixing + mixing_above + surface_row
    tracer_ids = lax.broadcasted_iota(jnp.int32, (1, tracers.shape[2], 1), 1)
    targets = (surface_patch[:, None, :] == tracer_ids).astype(jnp.float32)
    right_side = advected + surface_row[:, :, None] * targets[None]

    def forward(carry, layer):
        ratio_prev, value_prev = carry
        lower_band, diag_now, upper_band, right_now = layer
        pivot_now = diag_now - lower_band * ratio_prev
        ratio_now = upper_band / pivot_now
        value_now = (right_now - lower_band[:, None] * value_prev) / pivot_now[:, None]
        return ((ratio_now, value_now), (ratio_now, value_now))

    start_carry = (
        jnp.zeros(mixing.shape[1:], jnp.float32),
        jnp.zeros(tracers.shape[1:], jnp.float32),
    )
    ignored, (ratios, values) = lax.scan(
        forward, start_carry, (-mixing_above, diagonal, -mixing, right_side)
    )

    def backward(following, layer):
        ratio_now, value_now = layer
        solved_now = value_now - ratio_now[:, None] * following
        return (solved_now, solved_now)

    ignored_too, solved = lax.scan(
        backward, jnp.zeros(tracers.shape[1:], jnp.float32), (ratios, values), reverse=True
    )
    return solved


def local(
    tracers,
    vertical_speed,
    diffusivity,
    buoyancy_force,
    wet_levels,
    surface_patch,
    prior_height,
    land_mask,
    baroclinic_map,
    barotropic_map,
):
    blocks = wet_levels.shape[0]
    block_rows = land_mask.shape[1]
    block_cols = land_mask.shape[2]
    levels = vertical_speed.shape[0]
    band_row = lax.axis_index("by")
    column = lax.axis_index("bx")
    band_width = blocks * lax.axis_size("bx")
    band_first_slot = band_row * band_width
    clinic_band = (
        lax.dynamic_slice_in_dim(baroclinic_map, band_first_slot, band_width) - band_first_slot
    )
    tropic_band = (
        lax.dynamic_slice_in_dim(barotropic_map, band_first_slot, band_width) - band_first_slot
    )
    my_columns = lax.dynamic_slice_in_dim(tropic_band, column * blocks, blocks)
    depth_index = lax.broadcasted_iota(jnp.int32, buoyancy_force.shape, 0)
    wet_level = (depth_index < wet_levels[None]).astype(jnp.float32)
    forcing = jnp.sum(wet_level * buoyancy_force.astype(jnp.float32), axis=0)
    payload = jnp.stack([forcing, wet_levels.astype(jnp.float32), prior_height], axis=0)
    selector = (clinic_band[None, :] == my_columns[:, None]).astype(jnp.float32)
    relaid = jnp.einsum(
        "jt,qtc->qjc",
        selector,
        lax.all_gather(payload, "bx", axis=1, tiled=True),
        precision=PRECISE,
    )
    new_tracers = column_step(tracers, vertical_speed, diffusivity, wet_levels, surface_patch)
    shape_flat = (blocks, block_rows, block_cols)
    ocean_mask = land_mask.astype(jnp.float32)
    depth_field = relaid[1].reshape(shape_flat)
    source = ocean_mask * relaid[0].reshape(shape_flat)
    first_guess = ocean_mask * relaid[2].reshape(shape_flat)
    west_pick = (tropic_band[None, :] == (my_columns[:, None] - 1) % band_width).astype(jnp.float32)
    east_pick = (tropic_band[None, :] == (my_columns[:, None] + 1) % band_width).astype(jnp.float32)
    band_slots = lax.broadcasted_iota(jnp.int32, (band_width, 1), 0)
    geo_pick = (tropic_band[None, :] == band_slots).astype(jnp.float32)
    my_pick = (band_slots[:, 0][None, :] == my_columns[:, None]).astype(jnp.float32)

    def extend(field_blocks):
        edge_cols = jnp.stack([field_blocks[..., 0], field_blocks[..., -1]], axis=2)
        edge_rows = jnp.stack([field_blocks[..., 0, :], field_blocks[..., -1, :]], axis=2)
        gathered_cols, gathered_rows = (
            lax.all_gather(edge_cols, "bx", axis=1, tiled=True),
            lax.all_gather(edge_rows, "bx", axis=1, tiled=True),
        )
        geo_rows = jnp.einsum("ct,qtsw->sqcw", geo_pick, gathered_rows, precision=PRECISE)
        beside = padded_2(geo_rows, (("by", 0),), 1)
        north_side = jnp.einsum("jc,qcw->qjw", my_pick, beside[0], precision=PRECISE)
        south_side = jnp.einsum("jc,qcw->qjw", my_pick, beside[3], precision=PRECISE)
        west_side = jnp.einsum("jt,qth->qjh", west_pick, gathered_cols[:, :, 1], precision=PRECISE)
        east_side = jnp.einsum("jt,qth->qjh", east_pick, gathered_cols[:, :, 0], precision=PRECISE)
        middle = jnp.concatenate([west_side[..., None], field_blocks, east_side[..., None]], axis=3)
        north_row = jnp.pad(north_side, ((0, 0), (0, 0), (1, 1)))[:, :, None, :]
        south_row = jnp.pad(south_side, ((0, 0), (0, 0), (1, 1)))[:, :, None, :]
        return jnp.concatenate([north_row, middle, south_row], axis=2)

    statics = extend(jnp.stack([depth_field, ocean_mask], axis=0))
    depth_padded = statics[0]
    ocean_padded = statics[1]
    face_factor = FACE_SCALE / levels

    def face_weight(depth_other, ocean_other):
        return face_factor * jnp.minimum(depth_field, depth_other) * ocean_mask * ocean_other

    east_face = face_weight(depth_padded[:, 1:-1, 2:], ocean_padded[:, 1:-1, 2:])
    west_face = face_weight(depth_padded[:, 1:-1, :-2], ocean_padded[:, 1:-1, :-2])
    south_face = face_weight(depth_padded[:, 2:, 1:-1], ocean_padded[:, 2:, 1:-1])
    north_face = face_weight(depth_padded[:, :-2, 1:-1], ocean_padded[:, :-2, 1:-1])
    centre_weight = SURFACE * ocean_mask + (1.0 - ocean_mask)
    precond_diagonal = centre_weight + east_face + west_face + south_face + north_face

    def operate(field_blocks):
        padded = extend(field_blocks[None])[0]
        centre = centre_weight * field_blocks
        result = centre + east_face * (field_blocks - padded[:, 1:-1, 2:])
        result = result + west_face * (field_blocks - padded[:, 1:-1, :-2])
        result = result + south_face * (field_blocks - padded[:, 2:, 1:-1])
        return result + north_face * (field_blocks - padded[:, :-2, 1:-1])

    solution = first_guess
    residual = source - operate(solution)
    precond = residual / precond_diagonal

    def weighted(residual_now, precond_now):
        return lax.psum(jnp.sum(residual_now * precond_now), ("by", "bx"))

    direction = precond
    norm_now = weighted(residual, precond)
    for step_index in range(ITERS):
        image_field = operate(direction)
        step_size = norm_now / lax.psum(jnp.sum(direction * image_field), ("by", "bx"))
        solution = solution + step_size * direction
        residual = residual - step_size * image_field
        if step_index + 1 < ITERS:
            precond = residual / precond_diagonal
            norm_next = weighted(residual, precond)
            direction = precond + norm_next / norm_now * direction
            norm_now = norm_next
    return (new_tracers, solution)


def solution(mesh):
    return jax.shard_map(
        local,
        mesh=mesh,
        in_specs=(
            P(None, ("by", "bx"), None, None),
            P(None, ("by", "bx"), None),
            P(None, ("by", "bx"), None),
            P(None, ("by", "bx"), None),
            P(("by", "bx"), None),
            P(("by", "bx"), None),
            P(("by", "bx"), None),
            P(("by", "bx"), None, None),
            P(),
            P(),
        ),
        out_specs=(P(None, ("by", "bx"), None, None), P(("by", "bx"), None, None)),
        check_vma=False,
    )
```

profile of v0, /device:TPU:1, one launch (start us, length us, event | category | flops | bytes accessed | tf_op | source)
XLA Modules:
  0.0 1332.6 jit_solution(10514332008034676761)
XLA Ops:
  59.9 58.2 %while.34 = (s32[]{:T(128)}, f32[4,2048]{1,0:T(4,128)S(1)}, f32[4,16,2048]{2,1,0:T(8,128)S(1)}, f32[20,4,2048]{2,1,0:T(4,128)S(1)}, f32[20,4,16,2048]{3,2,1,0:T(...) while((s32[]{:T(128)}, f32[4,2048]{1,0:T(4,128)S(1)}, ...), condition=%wide.region_1.2_spmd.clone, body=%wide.region_0.0_spmd.clone.sunk | while | flops 557059 | bytes 2425468 | solution.py:55
  123.1 19.4 %all_gather.55 = f32[1,64,2,16]{3,2,0,1:T(2,128)S(1)} all-gather(f32[1,4,2,16]{3,2,0,1:T(2,128)S(1)} %copy.201), channel_id=1, replica_groups=mesh['by'=8,'bx'=16] {'bx'}, dimensions={1}, use_global_device_ids=true | all-gather | bytes 8704 | tf_op jit(solution)/shard_map/all_gather | solution.py:124
  142.9 17.5 %all_gather.54 = f32[1,64,2,128]{3,2,0,1:T(2,128)S(1)} all-gather(f32[1,4,2,128]{3,2,0,1:T(2,128)S(1)} %maximum_bitcast_fusion.7), channel_id=1, replica_groups=mesh['by'=8,'bx'=16] {'bx'}, dimensions={1}, use_global_device_ids=true | all-gather | bytes 69632 | tf_op jit(solution)/shard_map/all_gather | solution.py:125
  193.9 17.6 %all_gather.52 = f32[2,64,2,128]{3,2,0,1:T(2,128)S(1)} all-gather(f32[2,4,2,128]{3,2,0,1:T(2,128)S(1)} %fusion.130), channel_id=1, replica_groups=mesh['by'=8,'bx'=16] {'bx'}, dimensions={1}, use_global_device_ids=true | all-gather | bytes 139264 | tf_op jit(solution)/shard_map/all_gather | solution.py:125
  233.5 16.3 %all_gather.57 = f32[1,64,2,16]{3,2,0,1:T(2,128)S(1)} all-gather(f32[1,4,2,16]{3,2,0,1:T(2,128)S(1)} %copy.208), channel_id=1, replica_groups=mesh['by'=8,'bx'=16] {'bx'}, dimensions={1}, use_global_device_ids=true | all-gather | bytes 8704 | tf_op jit(solution)/shard_map/all_gather | solution.py:124
  250.1 17.4 %all_gather.56 = f32[1,64,2,128]{3,2,0,1:T(2,128)S(1)} all-gather(f32[1,4,2,128]{3,2,0,1:T(2,128)S(1)} %maximum_bitcast_fusion.8), channel_id=1, replica_groups=mesh['by'=8,'bx'=16] {'bx'}, dimensions={1}, use_global_device_ids=true | all-gather | bytes 69632 | tf_op jit(solution)/shard_map/all_gather | solution.py:125
  287.4 63.4 %all-reduce.19 = (f32[]{:T(128)}, f32[]{:T(128)}) all-reduce(f32[]{:T(128)} %get-tuple-element.217, f32[]{:T(128)} %get-tuple-element.216), channel_id=1, replica_groups=mesh['by'=8,'bx'=16] {'by','bx'}, use_global_device_ids=true, to_apply=%region_6.7 | all-reduce | flops 2 | bytes 16 | tf_op jit(solution)/shard_map/psum | solution.py:166
  352.7 63.8 %psum.86 = f32[]{:T(128)} all-reduce(f32[]{:T(128)} %get-tuple-element.276), channel_id=1, replica_groups=mesh['by'=8,'bx'=16] {'by','bx'}, use_global_device_ids=true, to_apply=%region_10.11 | all-reduce | flops 1 | bytes 8 | tf_op jit(solution)/shard_map/psum | solution.py:166
  434.3 17.6 %all_gather.58 = f32[1,64,2,128]{3,2,0,1:T(2,128)S(1)} all-gather(f32[1,4,2,128]{3,2,0,1:T(2,128)S(1)} %maximum_bitcast_fusion.9), channel_id=1, replica_groups=mesh['by'=8,'bx'=16] {'bx'}, dimensions={1}, use_global_device_ids=true | all-gather | bytes 69632 | tf_op jit(solution)/shard_map/all_gather | solution.py:125
  472.4 63.4 %psum.87 = f32[]{:T(128)} all-reduce(f32[]{:T(128)} %get-tuple-element.274), channel_id=1, replica_groups=mesh['by'=8,'bx'=16] {'by','bx'}, use_global_device_ids=true, to_apply=%region_12.13 | all-reduce | flops 1 | bytes 8 | tf_op jit(solution)/shard_map/psum | solution.py:172
  537.7 62.6 %psum.88 = f32[]{:T(128)} all-reduce(f32[]{:T(128)} %get-tuple-element.271), channel_id=1, replica_groups=mesh['by'=8,'bx'=16] {'by','bx'}, use_global_device_ids=true, to_apply=%region_14.15 | all-reduce | flops 1 | bytes 8 | tf_op jit(solution)/shard_map/psum | solution.py:166
  601.9 17.5 %all_gather.61 = f32[1,64,2,16]{3,2,0,1:T(2,128)S(1)} all-gather(f32[1,4,2,16]{3,2,0,1:T(2,128)S(1)} %copy.222), channel_id=1, replica_groups=mesh['by'=8,'bx'=16] {'bx'}, dimensions={1}, use_global_device_ids=true | all-gather | bytes 8704 | tf_op jit(solution)/shard_map/all_gather | solution.py:124
  657.8 62.1 %psum.89 = f32[]{:T(128)} all-reduce(f32[]{:T(128)} %get-tuple-element.269), channel_id=1, replica_groups=mesh['by'=8,'bx'=16] {'by','bx'}, use_global_device_ids=true, to_apply=%region_16.17 | all-reduce | flops 1 | bytes 8 | tf_op jit(solution)/shard_map/psum | solution.py:172
  721.9 64.2 %psum.90 = f32[]{:T(128)} all-reduce(f32[]{:T(128)} %get-tuple-element.266), channel_id=1, replica_groups=mesh['by'=8,'bx'=16] {'by','bx'}, use_global_device_ids=true, to_apply=%region_18.19 | all-reduce | flops 1 | bytes 8 | tf_op jit(solution)/shard_map/psum | solution.py:166
  787.6 16.1 %all_gather.63 = f32[1,64,2,16]{3,2,0,1:T(2,128)S(1)} all-gather(f32[1,4,2,16]{3,2,0,1:T(2,128)S(1)} %copy.229), channel_id=1, replica_groups=mesh['by'=8,'bx'=16] {'bx'}, dimensions={1}, use_global_device_ids=true | all-gather | bytes 8704 | tf_op jit(solution)/shard_map/all_gather | solution.py:124
  804.0 17.5 %all_gather.62 = f32[1,64,2,128]{3,2,0,1:T(2,128)S(1)} all-gather(f32[1,4,2,128]{3,2,0,1:T(2,128)S(1)} %maximum_bitcast_fusion.11), channel_id=1, replica_groups=mesh['by'=8,'bx'=16] {'bx'}, dimensions={1}, use_global_device_ids=true | all-gather | bytes 69632 | tf_op jit(solution)/shard_map/all_gather | solution.py:125
  841.0 64.5 %psum.91 = f32[]{:T(128)} all-reduce(f32[]{:T(128)} %get-tuple-element.264), channel_id=1, replica_groups=mesh['by'=8,'bx'=16] {'by','bx'}, use_global_device_ids=true, to_apply=%region_20.21 | all-reduce | flops 1 | bytes 8 | tf_op jit(solution)/shard_map/psum | solution.py:172
  907.5 62.5 %psum.92 = f32[]{:T(128)} all-reduce(f32[]{:T(128)} %get-tuple-element.261), channel_id=1, replica_groups=mesh['by'=8,'bx'=16] {'by','bx'}, use_global_device_ids=true, to_apply=%region_22.23 | all-reduce | flops 1 | bytes 8 | tf_op jit(solution)/shard_map/psum | solution.py:166
  971.5 17.6 %all_gather.65 = f32[1,64,2,16]{3,2,0,1:T(2,128)S(1)} all-gather(f32[1,4,2,16]{3,2,0,1:T(2,128)S(1)} %copy.236), channel_id=1, replica_groups=mesh['by'=8,'bx'=16] {'bx'}, dimensions={1}, use_global_device_ids=true | all-gather | bytes 8704 | tf_op jit(solution)/shard_map/all_gather | solution.py:124
  1027.3 62.1 %psum.93 = f32[]{:T(128)} all-reduce(f32[]{:T(128)} %get-tuple-element.259), channel_id=1, replica_groups=mesh['by'=8,'bx'=16] {'by','bx'}, use_global_device_ids=true, to_apply=%region_24.25 | all-reduce | flops 1 | bytes 8 | tf_op jit(solution)/shard_map/psum | solution.py:172
  1091.5 64.2 %psum.94 = f32[]{:T(128)} all-reduce(f32[]{:T(128)} %multiply_reduce_fusion), channel_id=1, replica_groups=mesh['by'=8,'bx'=16] {'by','bx'}, use_global_device_ids=true, to_apply=%region_26.27 | all-reduce | flops 1 | bytes 8 | tf_op jit(solution)/shard_map/psum | solution.py:166
  1173.6 17.5 %all_gather.66 = f32[1,64,2,128]{3,2,0,1:T(2,128)S(1)} all-gather(f32[1,4,2,128]{3,2,0,1:T(2,128)S(1)} %maximum_bitcast_fusion.13), channel_id=1, replica_groups=mesh['by'=8,'bx'=16] {'bx'}, dimensions={1}, use_global_device_ids=true | all-gather | bytes 69632 | tf_op jit(solution)/shard_map/all_gather | solution.py:125
  1216.1 43.3 %while.35 = (s32[]{:T(128)}, f32[4,16,2048]{2,1,0:T(8,128)S(1)}, f32[20,4,16,2048]{3,2,1,0:T(8,128)}, f32[20,4,16,2048]{3,2,1,0:T(8,128)}, f32[20,4,2048]{2,1,0:T(4,128)S(1)}, /*index=5*/s32[]{:T(128)}, s32[]{:T(128)}, s32[]{:T(128)}) while((s32[]{:T(128)}, f32[4,16,2048]{2,1,0:T(8,128)S(1)}, f32[20,4,16,2048]{3,2,1,0:T(8,128)}, ...), condition=%wide.region_3.4_spmd.clone, body=%wide.region_2.3_spmd.clone.sunk | while | flops 393220 | bytes 2195571 | solution.py:64
  1259.4 64.3 %psum.95 = f32[]{:T(128)} all-reduce(f32[]{:T(128)} %fusion.39), channel_id=1, replica_groups=mesh['by'=8,'bx'=16] {'by','bx'}, use_global_device_ids=true, to_apply=%region_28.29 | all-reduce | flops 1 | bytes 8 | tf_op jit(solution)/shard_map/psum | solution.py:172
  (330 shorter events, 413.6 us)
Async XLA Ops:
  7.2 112.6 %all-gather.2.cloned.1.call-start = ((), (), s32[]{:S(2)}) async-start(), calls=%async_computation | async-start | bytes 2228224 | tf_op jit(solution)/shard_map/all_gather | solution.py:105
  16.1 3.8 slice-start
  29.7 9.2 copy-start.1
  54.4 65.2 %copy-start = (s32[4,16,128]{2,1,0:T(8,128)S(1)}, s32[4,16,128]{2,1,0:T(8,128)}, u32[]{:S(2)}) copy-start(s32[4,16,128]{2,1,0:T(8,128)} %param.21) | copy-start | bytes 98308
  160.6 68.4 %collective-permute-start.2 = (f32[1,1,64,128]{3,2,0,1:T(8,128)S(1)}, f32[1,1,64,128]{3,2,0,1:T(8,128)S(1)}, u32[]{:S(2)}, u32[]{:S(2)}) collective-permute-start(f32[1,1,64,128]{3,2,0,1:T(8,128)S(1)} %get-tuple-element.331), channel_id=1, source_target_pairs={{0,16},{16,32},{32,48},{48,64},{64,80},{80,96},{96,112},{1,17},{17... | collective-permute-start | bytes 98312 | tf_op jit(solution)/shard_map/ppermute | solution.py:18
  175.2 54.1 %collective-permute-start.3 = (f32[1,1,64,128]{3,2,0,1:T(8,128)S(1)}, f32[1,1,64,128]{3,2,0,1:T(8,128)S(1)}, u32[]{:S(2)}, u32[]{:S(2)}) collective-permute-start(f32[1,1,64,128]{3,2,0,1:T(8,128)S(1)} %get-tuple-element.332), channel_id=1, source_target_pairs={{16,0},{32,16},{48,32},{64,48},{80,64},{96,80},{112,96},{17,1},{33... | collective-permute-start | bytes 98312 | tf_op jit(solution)/shard_map/ppermute | solution.py:21
  212.5 17.2 %collective-permute-start = (f32[1,2,64,128]{3,2,0,1:T(8,128)S(1)}, f32[1,2,64,128]{3,2,0,1:T(8,128)S(1)}, u32[]{:S(2)}, u32[]{:S(2)}) collective-permute-start(f32[1,2,64,128]{3,2,0,1:T(8,128)S(1)} %get-tuple-element.298), channel_id=1, source_target_pairs={{0,16},{16,32},{32,48},{48,64},{64,80},{80,96},{96,112},{1,17},{17... | collective-permute-start | bytes 196616 | tf_op jit(solution)/shard_map/ppermute | solution.py:18
  227.1 5.6 collective-permute-start.1
  267.7 15.3 %collective-permute-start.4 = (f32[1,1,64,128]{3,2,0,1:T(8,128)S(1)}, f32[1,1,64,128]{3,2,0,1:T(8,128)S(1)}, u32[]{:S(2)}, u32[]{:S(2)}) collective-permute-start(f32[1,1,64,128]{3,2,0,1:T(8,128)S(1)} %get-tuple-element.325), channel_id=1, source_target_pairs={{0,16},{16,32},{32,48},{48,64},{64,80},{80,96},{96,112},{1,17},{17... | collective-permute-start | bytes 98312 | tf_op jit(solution)/shard_map/ppermute | solution.py:18
  281.0 5.2 collective-permute-start.5
  452.1 15.9 %collective-permute-start.6 = (f32[1,1,64,128]{3,2,0,1:T(8,128)S(1)}, f32[1,1,64,128]{3,2,0,1:T(8,128)S(1)}, u32[]{:S(2)}, u32[]{:S(2)}) collective-permute-start(f32[1,1,64,128]{3,2,0,1:T(8,128)S(1)} %get-tuple-element.321), channel_id=1, source_target_pairs={{0,16},{16,32},{32,48},{48,64},{64,80},{80,96},{96,112},{1,17},{17... | collective-permute-start | bytes 98312 | tf_op jit(solution)/shard_map/ppermute | solution.py:18
  466.0 5.2 collective-permute-start.7
  635.9 17.5 %collective-permute-start.8 = (f32[1,1,64,128]{3,2,0,1:T(8,128)S(1)}, f32[1,1,64,128]{3,2,0,1:T(8,128)S(1)}, u32[]{:S(2)}, u32[]{:S(2)}) collective-permute-start(f32[1,1,64,128]{3,2,0,1:T(8,128)S(1)} %get-tuple-element.317), channel_id=1, source_target_pairs={{0,16},{16,32},{32,48},{48,64},{64,80},{80,96},{96,112},{1,17},{17... | collective-permute-start | bytes 98312 | tf_op jit(solution)/shard_map/ppermute | solution.py:18
  651.5 5.2 collective-permute-start.9
  821.6 15.7 %collective-permute-start.10 = (f32[1,1,64,128]{3,2,0,1:T(8,128)S(1)}, f32[1,1,64,128]{3,2,0,1:T(8,128)S(1)}, u32[]{:S(2)}, u32[]{:S(2)}) collective-permute-start(f32[1,1,64,128]{3,2,0,1:T(8,128)S(1)} %get-tuple-element.313), channel_id=1, source_target_pairs={{0,16},{16,32},{32,48},{48,64},{64,80},{80,96},{96,112},{1,17},{17... | collective-permute-start | bytes 98312 | tf_op jit(solution)/shard_map/ppermute | solution.py:18
  834.7 5.2 collective-permute-start.11
  1005.6 17.4 %collective-permute-start.12 = (f32[1,1,64,128]{3,2,0,1:T(8,128)S(1)}, f32[1,1,64,128]{3,2,0,1:T(8,128)S(1)}, u32[]{:S(2)}, u32[]{:S(2)}) collective-permute-start(f32[1,1,64,128]{3,2,0,1:T(8,128)S(1)} %get-tuple-element.309), channel_id=1, source_target_pairs={{0,16},{16,32},{32,48},{48,64},{64,80},{80,96},{96,112},{1,17},{17... | collective-permute-start | bytes 98312 | tf_op jit(solution)/shard_map/ppermute | solution.py:18
  1021.0 5.2 collective-permute-start.13
  1191.3 15.7 %collective-permute-start.14 = (f32[1,1,64,128]{3,2,0,1:T(8,128)S(1)}, f32[1,1,64,128]{3,2,0,1:T(8,128)S(1)}, u32[]{:S(2)}, u32[]{:S(2)}) collective-permute-start(f32[1,1,64,128]{3,2,0,1:T(8,128)S(1)} %get-tuple-element.305), channel_id=1, source_target_pairs={{0,16},{16,32},{32,48},{48,64},{64,80},{80,96},{96,112},{1,17},{17... | collective-permute-start | bytes 98312 | tf_op jit(solution)/shard_map/ppermute | solution.py:18
  1204.3 5.2 collective-permute-start.15
Sparse Core Ops, SparseCore 0:
  15.3 46.3 all-gather.1
where the time goes:
time: 1340 us; the launch traced here: 1330 us
  blocking collectives  969 us (72%)
  other arithmetic  146 us (11%)
  starting transfers between devices  128 us (10%)
  local copies, waits for them, and re-layouts  29.9 us (2%)
  between operations  29.7 us (2%)
  waiting for transfers between devices  19.4 us (1%)
    psum x6, blocking collectives, weighted(): return lax.psum(jnp.sum(residual_now * precond_now), ('by', 'bx'))  381 us
    psum x5, blocking collectives, local(): lax.psum(jnp.sum(direction * image_field), ('by', 'bx'))  317 us
    all_gather x8, blocking collectives, extend(): lax.all_gather(edge_rows, 'bx', axis=1, tiled=True)  137 us
    all_gather x8, blocking collectives, extend(): lax.all_gather(edge_cols, 'bx', axis=1, tiled=True)  135 us
    ppermute x8, starting transfers between devices, padded_2(): lax.ppermute(lax.slice_in_dim(block, block.shape[dim] - width, None, axis...  111 us
    dynamic_update_slice x60, other arithmetic, column_step(): lax.scan(forward, start_carry, (-mixing_above, diagonal, -mixing, right_s...  101 us
  transfers between devices with their start and end apart: 17, of which 7 were waited for; matrix products, arithmetic and copies ran while one was open for 8% of the time, Pallas kernels for 0%

commit v1 on v0

--- a/solution.py
+++ b/solution.py
@@ -8,6 +8,11 @@
 SURFACE = 0.1
 FACE_SCALE = 2.0
 PRECISE = lax.Precision.HIGHEST
+
+
+def swapped_in(shard, axis, along):
+    sent = jnp.stack([shard] * lax.axis_size(axis))
+    return jnp.concatenate(lax.all_to_all(sent, axis, 0, 0), axis=along)
 
 
 def padded_2(block, sides, width):
@@ -121,7 +126,7 @@
         edge_cols = jnp.stack([field_blocks[..., 0], field_blocks[..., -1]], axis=2)
         edge_rows = jnp.stack([field_blocks[..., 0, :], field_blocks[..., -1, :]], axis=2)
         gathered_cols, gathered_rows = (
-            lax.all_gather(edge_cols, "bx", axis=1, tiled=True),
+            swapped_in(edge_cols, "bx", 1),
             lax.all_gather(edge_rows, "bx", axis=1, tiled=True),
         )
         geo_rows = jnp.einsum("ct,qtsw->sqcw", geo_pick, gathered_rows, precision=PRECISE)

time: 1340 us -> 1220 us (0.910)
  blocking collectives: 969 us -> 842 us
    all_gather x8 -> x0, blocking collectives: 135 us -> none  [extend(): lax.all_gather(edge_cols, 'bx', axis=1, tiled=True)]
    ppermute x8, starting transfers between devices: 111 us -> 75.2 us  [padded_2(): lax.ppermute(lax.slice_in_dim(block, block.shape[dim] - width, None, axis...]
    all_to_all x0 -> x8, starting transfers between devices: none -> 35.9 us  [swapped_in(): return jnp.concatenate(lax.all_to_all(sent, axis, 0, 0), axis=along)]
  transfers between devices with their start and end apart: 17 -> 25, of which waited for: 7 -> 7; matrix products, arithmetic and copies ran while one was open for 8% -> 10% of each run, Pallas kernels for 0% -> 0%
where the time goes in v1:
time: 1220 us; the launch traced here: 1210 us
  blocking collectives  842 us (69%)
  other arithmetic  151 us (12%)
  starting transfers between devices  127 us (10%)
  local copies, waits for them, and re-layouts  37.3 us (3%)
  between operations  29.7 us (2%)
  waiting for transfers between devices  13.7 us (1%)
    psum x6, blocking collectives, weighted(): return lax.psum(jnp.sum(residual_now * precond_now), ('by', 'bx'))  378 us
    psum x5, blocking collectives, local(): lax.psum(jnp.sum(direction * image_field), ('by', 'bx'))  318 us
    all_gather x8, blocking collectives, extend(): lax.all_gather(edge_rows, 'bx', axis=1, tiled=True)  146 us
    dynamic_update_slice x60, other arithmetic, column_step(): lax.scan(forward, start_carry, (-mixing_above, diagonal, -mixing, right_s...  101 us
    ppermute x8, starting transfers between devices, padded_2(): lax.ppermute(lax.slice_in_dim(block, block.shape[dim] - width, None, axis...  75.2 us
    all_to_all x8, starting transfers between devices, swapped_in(): return jnp.concatenate(lax.all_to_all(sent, axis, 0, 0), axis=along)  35.9 us
  transfers between devices with their start and end apart: 25, of which 7 were waited for; matrix products, arithmetic and copies ran while one was open for 10% of the time, Pallas kernels for 0%

profile of v1, /device:TPU:1, one launch (start us, length us, event | category | flops | bytes accessed | tf_op | source)
XLA Modules:
  0.0 1210.8 jit_solution(6045640837604264747)
XLA Ops:
  19.9 9.8 multiply_add_fusion.1
  38.9 15.5 %multiply_add_fusion = f32[20,4,16,2048]{3,2,1,0:T(8,128)} fusion(f32[19,4,16,2048]{3,2,1,0:T(8,128)} %slice.433, f32[20,4,16,2048]{3,2,1,0:T(8,128)} %param.14, f32[20,4,16,2048]{3,2,1,0:T(8,128)} %multiply_add_fusion.1, f32[4,16,2048]{2,1,0:T(8,128)S(1)} %fusion.3, f32[20,4,2048]{2,1,0:T(4,128)S(1)} %get-tuple-element.335, f32[20,4,2048]{2,1,0:T(4,128)S(1)} %fusion.2), kind=kLoop, calls=%fused_computation.13 | loop fusion | flops 13107200 | bytes 43253760 | tf_op jit(solution)/shard_map/add | solution.py:46
  59.9 58.2 %while.34 = (s32[]{:T(128)}, f32[4,2048]{1,0:T(4,128)S(1)}, f32[4,16,2048]{2,1,0:T(8,128)S(1)}, f32[20,4,2048]{2,1,0:T(4,128)S(1)}, f32[20,4,16,2048]{3,2,1,0:T(...) while((s32[]{:T(128)}, f32[4,2048]{1,0:T(4,128)S(1)}, ...), condition=%wide.region_1.2_spmd.clone, body=%wide.region_0.0_spmd.clone.sunk | while | flops 557059 | bytes 2425468 | solution.py:60
  131.5 18.3 %all_gather.29 = f32[1,64,2,128]{3,2,0,1:T(2,128)S(1)} all-gather(f32[1,4,2,128]{3,2,0,1:T(2,128)S(1)} %maximum_bitcast_fusion.7), channel_id=1, replica_groups=mesh['by'=8,'bx'=16] {'bx'}, dimensions={1}, use_global_device_ids=true | all-gather | bytes 69632 | tf_op jit(solution)/shard_map/all_gather | solution.py:130
  162.0 17.5 %all_gather.28 = f32[2,64,2,128]{3,2,0,1:T(2,128)S(1)} all-gather(f32[2,4,2,128]{3,2,0,1:T(2,128)S(1)} %fusion.128), channel_id=1, replica_groups=mesh['by'=8,'bx'=16] {'bx'}, dimensions={1}, use_global_device_ids=true | all-gather | bytes 139264 | tf_op jit(solution)/shard_map/all_gather | solution.py:130
  209.5 18.5 %all_gather.30 = f32[1,64,2,128]{3,2,0,1:T(2,128)S(1)} all-gather(f32[1,4,2,128]{3,2,0,1:T(2,128)S(1)} %maximum_bitcast_fusion.8), channel_id=1, replica_groups=mesh['by'=8,'bx'=16] {'bx'}, dimensions={1}, use_global_device_ids=true | all-gather | bytes 69632 | tf_op jit(solution)/shard_map/all_gather | solution.py:130
  228.1 10.8 collective-permute-start.4
  245.3 64.4 %all-reduce.19 = (f32[]{:T(128)}, f32[]{:T(128)}) all-reduce(f32[]{:T(128)} %get-tuple-element.219, f32[]{:T(128)} %get-tuple-element.218), channel_id=1, replica_groups=mesh['by'=8,'bx'=16] {'by','bx'}, use_global_device_ids=true, to_apply=%region_6.7 | all-reduce | flops 2 | bytes 16 | tf_op jit(solution)/shard_map/psum | solution.py:171
  311.7 62.9 %psum.86 = f32[]{:T(128)} all-reduce(f32[]{:T(128)} %get-tuple-element.278), channel_id=1, replica_groups=mesh['by'=8,'bx'=16] {'by','bx'}, use_global_device_ids=true, to_apply=%region_10.11 | all-reduce | flops 1 | bytes 8 | tf_op jit(solution)/shard_map/psum | solution.py:171
  380.7 18.3 %all_gather.31 = f32[1,64,2,128]{3,2,0,1:T(2,128)S(1)} all-gather(f32[1,4,2,128]{3,2,0,1:T(2,128)S(1)} %maximum_bitcast_fusion.9), channel_id=1, replica_groups=mesh['by'=8,'bx'=16] {'bx'}, dimensions={1}, use_global_device_ids=true | all-gather | bytes 69632 | tf_op jit(solution)/shard_map/all_gather | solution.py:130
  414.5 63.7 %psum.87 = f32[]{:T(128)} all-reduce(f32[]{:T(128)} %get-tuple-element.276), channel_id=1, replica_groups=mesh['by'=8,'bx'=16] {'by','bx'}, use_global_device_ids=true, to_apply=%region_12.13 | all-reduce | flops 1 | bytes 8 | tf_op jit(solution)/shard_map/psum | solution.py:177
  480.0 62.6 %psum.88 = f32[]{:T(128)} all-reduce(f32[]{:T(128)} %get-tuple-element.273), channel_id=1, replica_groups=mesh['by'=8,'bx'=16] {'by','bx'}, use_global_device_ids=true, to_apply=%region_14.15 | all-reduce | flops 1 | bytes 8 | tf_op jit(solution)/shard_map/psum | solution.py:171
  549.1 18.3 %all_gather.32 = f32[1,64,2,128]{3,2,0,1:T(2,128)S(1)} all-gather(f32[1,4,2,128]{3,2,0,1:T(2,128)S(1)} %maximum_bitcast_fusion.10), channel_id=1, replica_groups=mesh['by'=8,'bx'=16] {'bx'}, dimensions={1}, use_global_device_ids=true | all-gather | bytes 69632 | tf_op jit(solution)/shard_map/all_gather | solution.py:130
  582.9 63.7 %psum.89 = f32[]{:T(128)} all-reduce(f32[]{:T(128)} %get-tuple-element.271), channel_id=1, replica_groups=mesh['by'=8,'bx'=16] {'by','bx'}, use_global_device_ids=true, to_apply=%region_16.17 | all-reduce | flops 1 | bytes 8 | tf_op jit(solution)/shard_map/psum | solution.py:177
  648.6 62.6 %psum.90 = f32[]{:T(128)} all-reduce(f32[]{:T(128)} %get-tuple-element.268), channel_id=1, replica_groups=mesh['by'=8,'bx'=16] {'by','bx'}, use_global_device_ids=true, to_apply=%region_18.19 | all-reduce | flops 1 | bytes 8 | tf_op jit(solution)/shard_map/psum | solution.py:171
  717.7 18.3 %all_gather.33 = f32[1,64,2,128]{3,2,0,1:T(2,128)S(1)} all-gather(f32[1,4,2,128]{3,2,0,1:T(2,128)S(1)} %maximum_bitcast_fusion.11), channel_id=1, replica_groups=mesh['by'=8,'bx'=16] {'bx'}, dimensions={1}, use_global_device_ids=true | all-gather | bytes 69632 | tf_op jit(solution)/shard_map/all_gather | solution.py:130
  751.8 63.7 %psum.91 = f32[]{:T(128)} all-reduce(f32[]{:T(128)} %get-tuple-element.266), channel_id=1, replica_groups=mesh['by'=8,'bx'=16] {'by','bx'}, use_global_device_ids=true, to_apply=%region_20.21 | all-reduce | flops 1 | bytes 8 | tf_op jit(solution)/shard_map/psum | solution.py:177
  817.3 62.7 %psum.92 = f32[]{:T(128)} all-reduce(f32[]{:T(128)} %get-tuple-element.263), channel_id=1, replica_groups=mesh['by'=8,'bx'=16] {'by','bx'}, use_global_device_ids=true, to_apply=%region_22.23 | all-reduce | flops 1 | bytes 8 | tf_op jit(solution)/shard_map/psum | solution.py:171
  886.5 18.3 %all_gather.34 = f32[1,64,2,128]{3,2,0,1:T(2,128)S(1)} all-gather(f32[1,4,2,128]{3,2,0,1:T(2,128)S(1)} %maximum_bitcast_fusion.12), channel_id=1, replica_groups=mesh['by'=8,'bx'=16] {'bx'}, dimensions={1}, use_global_device_ids=true | all-gather | bytes 69632 | tf_op jit(solution)/shard_map/all_gather | solution.py:130
  920.5 63.7 %psum.93 = f32[]{:T(128)} all-reduce(f32[]{:T(128)} %get-tuple-element.261), channel_id=1, replica_groups=mesh['by'=8,'bx'=16] {'by','bx'}, use_global_device_ids=true, to_apply=%region_24.25 | all-reduce | flops 1 | bytes 8 | tf_op jit(solution)/shard_map/psum | solution.py:177
  986.2 62.7 %psum.94 = f32[]{:T(128)} all-reduce(f32[]{:T(128)} %multiply_reduce_fusion), channel_id=1, replica_groups=mesh['by'=8,'bx'=16] {'by','bx'}, use_global_device_ids=true, to_apply=%region_26.27 | all-reduce | flops 1 | bytes 8 | tf_op jit(solution)/shard_map/psum | solution.py:171
  1055.5 18.3 %all_gather.35 = f32[1,64,2,128]{3,2,0,1:T(2,128)S(1)} all-gather(f32[1,4,2,128]{3,2,0,1:T(2,128)S(1)} %maximum_bitcast_fusion.13), channel_id=1, replica_groups=mesh['by'=8,'bx'=16] {'bx'}, dimensions={1}, use_global_device_ids=true | all-gather | bytes 69632 | tf_op jit(solution)/shard_map/all_gather | solution.py:130
  1094.9 43.3 %while.35 = (s32[]{:T(128)}, f32[4,16,2048]{2,1,0:T(8,128)S(1)}, f32[20,4,16,2048]{3,2,1,0:T(8,128)}, f32[20,4,16,2048]{3,2,1,0:T(8,128)}, f32[20,4,2048]{2,1,0:T(4,128)S(1)}, /*index=5*/s32[]{:T(128)}, s32[]{:T(128)}, s32[]{:T(128)}) while((s32[]{:T(128)}, f32[4,16,2048]{2,1,0:T(8,128)S(1)}, f32[20,4,16,2048]{3,2,1,0:T(8,128)}, ...), condition=%wide.region_3.4_spmd.clone, body=%wide.region_2.3_spmd.clone.sunk | while | flops 393220 | bytes 2195571 | solution.py:69
  1138.3 63.7 %psum.95 = f32[]{:T(128)} all-reduce(f32[]{:T(128)} %fusion.39), channel_id=1, replica_groups=mesh['by'=8,'bx'=16] {'by','bx'}, use_global_device_ids=true, to_apply=%region_28.29 | all-reduce | flops 1 | bytes 8 | tf_op jit(solution)/shard_map/psum | solution.py:177
  (368 shorter events, 302.8 us)
Async XLA Ops:
  7.2 112.6 %all-gather.2.cloned.1.call-start = ((), (), s32[]{:S(2)}) async-start(), calls=%async_computation.8 | async-start | bytes 2228224 | tf_op jit(solution)/shard_map/all_gather | solution.py:110
  123.8 67.8 %all-to-all-start.1 = ((f32[16,1,128]{2,1,0:T(1,128)}), f32[16,1,128]{2,1,0:T(1,128)S(1)}, u32[]{:S(2)}, u32[]{:S(2)}) async-start(f32[16,1,128]{2,1,0:T(1,128)} %reshape.329), calls=%async_computation.1 | async-start | bytes 16384 | tf_op jit(solution)/shard_map/all_to_all | solution.py:15
  150.1 53.3 %collective-permute-start.2 = (f32[1,1,64,128]{3,2,0,1:T(8,128)S(1)}, f32[1,1,64,128]{3,2,0,1:T(8,128)S(1)}, u32[]{:S(2)}, u32[]{:S(2)}) collective-permute-start(f32[1,1,64,128]{3,2,0,1:T(8,128)S(1)} %get-tuple-element.331), channel_id=1, source_target_pairs={{0,16},{16,32},{32,48},{48,64},{64,80},{80,96},{96,112},{1,17},{17... | collective-permute-start | bytes 98312 | tf_op jit(solution)/shard_map/ppermute | solution.py:23
  159.8 43.9 %collective-permute-start.3 = (f32[1,1,64,128]{3,2,0,1:T(8,128)S(1)}, f32[1,1,64,128]{3,2,0,1:T(8,128)S(1)}, u32[]{:S(2)}, u32[]{:S(2)}) collective-permute-start(f32[1,1,64,128]{3,2,0,1:T(8,128)S(1)} %get-tuple-element.332), channel_id=1, source_target_pairs={{16,0},{32,16},{48,32},{64,48},{80,64},{96,80},{112,96},{17,1},{33... | collective-permute-start | bytes 98312 | tf_op jit(solution)/shard_map/ppermute | solution.py:26
  180.6 23.5 %collective-permute-start = (f32[1,2,64,128]{3,2,0,1:T(8,128)S(1)}, f32[1,2,64,128]{3,2,0,1:T(8,128)S(1)}, u32[]{:S(2)}, u32[]{:S(2)}) collective-permute-start(f32[1,2,64,128]{3,2,0,1:T(8,128)S(1)} %get-tuple-element.300), channel_id=1, source_target_pairs={{0,16},{16,32},{32,48},{48,64},{64,80},{80,96},{96,112},{1,17},{17... | collective-permute-start | bytes 196616 | tf_op jit(solution)/shard_map/ppermute | solution.py:23
  189.7 14.7 %collective-permute-start.1 = (f32[1,2,64,128]{3,2,0,1:T(8,128)S(1)}, f32[1,2,64,128]{3,2,0,1:T(8,128)S(1)}, u32[]{:S(2)}, u32[]{:S(2)}) collective-permute-start(f32[1,2,64,128]{3,2,0,1:T(8,128)S(1)} %get-tuple-element.301), channel_id=1, source_target_pairs={{16,0},{32,16},{48,32},{64,48},{80,64},{96,80},{112,96},{17,1},{33... | collective-permute-start | bytes 196616 | tf_op jit(solution)/shard_map/ppermute | solution.py:26
  191.6 10.2 all-to-all-start
  206.0 34.9 %all-to-all-start.2 = ((f32[16,1,128]{2,1,0:T(1,128)}), f32[16,1,128]{2,1,0:T(1,128)S(1)}, u32[]{:S(2)}, u32[]{:S(2)}) async-start(f32[16,1,128]{2,1,0:T(1,128)} %reshape.331), calls=%async_computation.2 | async-start | bytes 16384 | tf_op jit(solution)/shard_map/all_to_all | solution.py:15
  228.1 14.3 %collective-permute-start.4 = (f32[1,1,64,128]{3,2,0,1:T(8,128)S(1)}, f32[1,1,64,128]{3,2,0,1:T(8,128)S(1)}, u32[]{:S(2)}, u32[]{:S(2)}) collective-permute-start(f32[1,1,64,128]{3,2,0,1:T(8,128)S(1)} %get-tuple-element.325), channel_id=1, source_target_pairs={{0,16},{16,32},{32,48},{48,64},{64,80},{80,96},{96,112},{1,17},{17... | collective-permute-start | bytes 98312 | tf_op jit(solution)/shard_map/ppermute | solution.py:23
  239.0 5.2 collective-permute-start.5
  376.8 33.3 %all-to-all-start.3 = ((f32[16,1,128]{2,1,0:T(1,128)}), f32[16,1,128]{2,1,0:T(1,128)S(1)}, u32[]{:S(2)}, u32[]{:S(2)}) async-start(f32[16,1,128]{2,1,0:T(1,128)} %reshape.333), calls=%async_computation.3 | async-start | bytes 16384 | tf_op jit(solution)/shard_map/all_to_all | solution.py:15
  399.3 12.3 %collective-permute-start.6 = (f32[1,1,64,128]{3,2,0,1:T(8,128)S(1)}, f32[1,1,64,128]{3,2,0,1:T(8,128)S(1)}, u32[]{:S(2)}, u32[]{:S(2)}) collective-permute-start(f32[1,1,64,128]{3,2,0,1:T(8,128)S(1)} %get-tuple-element.321), channel_id=1, source_target_pairs={{0,16},{16,32},{32,48},{48,64},{64,80},{80,96},{96,112},{1,17},{17... | collective-permute-start | bytes 98312 | tf_op jit(solution)/shard_map/ppermute | solution.py:23
  408.1 5.2 collective-permute-start.7
  544.8 33.8 %all-to-all-start.4 = ((f32[16,1,128]{2,1,0:T(1,128)}), f32[16,1,128]{2,1,0:T(1,128)S(1)}, u32[]{:S(2)}, u32[]{:S(2)}) async-start(f32[16,1,128]{2,1,0:T(1,128)} %reshape.335), calls=%async_computation.4 | async-start | bytes 16384 | tf_op jit(solution)/shard_map/all_to_all | solution.py:15
  567.7 12.3 %collective-permute-start.8 = (f32[1,1,64,128]{3,2,0,1:T(8,128)S(1)}, f32[1,1,64,128]{3,2,0,1:T(8,128)S(1)}, u32[]{:S(2)}, u32[]{:S(2)}) collective-permute-start(f32[1,1,64,128]{3,2,0,1:T(8,128)S(1)} %get-tuple-element.317), channel_id=1, source_target_pairs={{0,16},{16,32},{32,48},{48,64},{64,80},{80,96},{96,112},{1,17},{17... | collective-permute-start | bytes 98312 | tf_op jit(solution)/shard_map/ppermute | solution.py:23
  713.4 34.3 %all-to-all-start.5 = ((f32[16,1,128]{2,1,0:T(1,128)}), f32[16,1,128]{2,1,0:T(1,128)S(1)}, u32[]{:S(2)}, u32[]{:S(2)}) async-start(f32[16,1,128]{2,1,0:T(1,128)} %reshape.337), calls=%async_computation.5 | async-start | bytes 16384 | tf_op jit(solution)/shard_map/all_to_all | solution.py:15
  736.3 12.8 %collective-permute-start.10 = (f32[1,1,64,128]{3,2,0,1:T(8,128)S(1)}, f32[1,1,64,128]{3,2,0,1:T(8,128)S(1)}, u32[]{:S(2)}, u32[]{:S(2)}) collective-permute-start(f32[1,1,64,128]{3,2,0,1:T(8,128)S(1)} %get-tuple-element.313), channel_id=1, source_target_pairs={{0,16},{16,32},{32,48},{48,64},{64,80},{80,96},{96,112},{1,17},{17... | collective-permute-start | bytes 98312 | tf_op jit(solution)/shard_map/ppermute | solution.py:23
  745.5 5.2 collective-permute-start.11
  882.2 33.9 %all-to-all-start.6 = ((f32[16,1,128]{2,1,0:T(1,128)}), f32[16,1,128]{2,1,0:T(1,128)S(1)}, u32[]{:S(2)}, u32[]{:S(2)}) async-start(f32[16,1,128]{2,1,0:T(1,128)} %reshape.339), calls=%async_computation.6 | async-start | bytes 16384 | tf_op jit(solution)/shard_map/all_to_all | solution.py:15
  905.0 12.6 %collective-permute-start.12 = (f32[1,1,64,128]{3,2,0,1:T(8,128)S(1)}, f32[1,1,64,128]{3,2,0,1:T(8,128)S(1)}, u32[]{:S(2)}, u32[]{:S(2)}) collective-permute-start(f32[1,1,64,128]{3,2,0,1:T(8,128)S(1)} %get-tuple-element.309), channel_id=1, source_target_pairs={{0,16},{16,32},{32,48},{48,64},{64,80},{80,96},{96,112},{1,17},{17... | collective-permute-start | bytes 98312 | tf_op jit(solution)/shard_map/ppermute | solution.py:23
  914.2 5.2 collective-permute-start.13
  1051.2 33.9 %all-to-all-start.7 = ((f32[16,1,128]{2,1,0:T(1,128)}), f32[16,1,128]{2,1,0:T(1,128)S(1)}, u32[]{:S(2)}, u32[]{:S(2)}) async-start(f32[16,1,128]{2,1,0:T(1,128)} %reshape.341), calls=%async_computation.7 | async-start | bytes 16384 | tf_op jit(solution)/shard_map/all_to_all | solution.py:15
  1074.0 12.6 %collective-permute-start.14 = (f32[1,1,64,128]{3,2,0,1:T(8,128)S(1)}, f32[1,1,64,128]{3,2,0,1:T(8,128)S(1)}, u32[]{:S(2)}, u32[]{:S(2)}) collective-permute-start(f32[1,1,64,128]{3,2,0,1:T(8,128)S(1)} %get-tuple-element.305), channel_id=1, source_target_pairs={{0,16},{16,32},{32,48},{48,64},{64,80},{80,96},{96,112},{1,17},{17... | collective-permute-start | bytes 98312 | tf_op jit(solution)/shard_map/ppermute | solution.py:23
  1083.2 5.2 collective-permute-start.15
  (4 other events, 83.5 us)
Sparse Core Ops, SparseCore 0:
  15.3 46.3 all-gather.1
